TPU v7x, 32 devices: a whole 2x2x4 slice. The times are simulated.
32 devices in a mesh: dp: 8 (over z, x), seq: 4 (over y, core).
Axes of the slice: x: 2, y: 2, z: 4, core: 2. Of those that a mesh axis runs over, the one named last changes fastest.
Arguments:
- queries: bfloat16 [8, 512, 2048], P('dp', 'seq'), may hold values from -72 to 72
- hit_keys: bfloat16 [8, 512, 2048], P('dp', 'seq'), may hold values from -12 to 12
- hit_values: bfloat16 [8, 512, 2048], P('dp', 'seq'), may hold values from -6 to 6
- hit_counts: int32 [8], P('dp'), may hold values from 128 to 512, as said below
- master_weight: float32 [8, 256, 2048], P('dp', None, 'seq'), may hold values from -0.5 to 0.5
- first_moment: float32 [8, 256, 2048], P('dp', None, 'seq'), may hold values from -4 to 4
- second_moment: float32 [8, 256, 2048], P('dp', None, 'seq'), may hold values from 0.1 to 4
- gradient: float32 [8, 256, 2048], P('dp', None, 'seq'), may hold values from -6 to 6
- owner_bucket: int32 [8], replicated, may hold values from 0 to 7, each once
Outputs:
- projected: bfloat16 [8, 512, 2048], P('dp', 'seq')
- new_master: float32 [8, 256, 2048], P('dp', None, 'seq')
- new_first: float32 [8, 256, 2048], P('dp', None, 'seq')
- new_second: float32 [8, 256, 2048], P('dp', None, 'seq')
Inputs may be any that keep to these rules, and one draw needn't show every extreme that they name: The valid hits of event e are its first hit_counts[e] slots; some event is full. `owner_bucket`: each bucket is held by exactly one owner.
All inputs are finite; a program needn't handle non-finite values.
Results may differ from a plain program's by a relative error of at most 0.0063.
Values may be sent and summed in bfloat16 or wider, within the bound.
No kernel may reach another device: no remote copies, remote signals or barrier semaphores. Data moves between devices by JAX's collectives and lax.ppermute only.
A program may use at most 64 MiB of HBM per device.

v0:
```python
import jax
import jax.numpy as jnp
from jax import lax
from jax.sharding import PartitionSpec as P

HEAD_DIM = 128
beta_one = 0.9
beta_two = 0.999
learn_rate = 0.003
weight_decay = 0.1
epsilon = 1e-08
step_count = 10.0
block_rows = 512


def adam_update(master_weight, first_moment, second_moment, gradient):
    new_first = beta_one * first_moment + (1.0 - beta_one) * gradient
    new_second = beta_two * second_moment + (1.0 - beta_two) * gradient * gradient
    first_hat = new_first / (1.0 - beta_one**step_count)
    second_hat = new_second / (1.0 - beta_two**step_count)
    new_master = master_weight - learn_rate * (
        first_hat / (jnp.sqrt(second_hat) + epsilon) + weight_decay * master_weight
    )
    return (new_master, new_first, new_second)


def attend_head(head_query, head_keys, head_values, count):
    length = head_query.shape[0]
    block = min(block_rows, length)
    scale = head_query.shape[1] ** (-0.5)
    valid = lax.broadcasted_iota(jnp.int32, (1, length), 1) < count

    def one_block(rows):
        scores = (
            lax.dot_general(
                rows, head_keys, (((1,), (1,)), ((), ())), preferred_element_type=jnp.float32
            )
            * scale
        )
        scores = jnp.where(valid, scores, -jnp.inf)
        top = jnp.max(scores, axis=1, keepdims=True)
        expo = jnp.exp(scores - top)
        weights = (expo / jnp.sum(expo, axis=1, keepdims=True)).astype(jnp.bfloat16)
        return jnp.dot(weights, head_values, preferred_element_type=jnp.float32).astype(
            jnp.bfloat16
        )

    blocks = head_query.reshape(length // block, block, head_query.shape[1])
    return lax.map(one_block, blocks).reshape(length, head_query.shape[1])


def body(
    queries,
    hit_keys,
    hit_values,
    hit_counts,
    master_weight,
    first_moment,
    second_moment,
    gradient,
    owner_bucket,
):
    new_master, new_first, new_second = adam_update(
        master_weight, first_moment, second_moment, gradient
    )
    weight_half = new_master.astype(jnp.bfloat16)
    groups = lax.axis_size("seq")
    owners = lax.axis_size("dp")
    tok_rows = queries.shape[1]
    width = queries.shape[2]
    per_group = width // groups
    heads_here = per_group // HEAD_DIM
    count = hit_counts[0]
    matches = owner_bucket[:, None] == jnp.arange(owners, dtype=jnp.int32)[None, :]
    inverse = jnp.sum(jnp.where(matches, jnp.arange(owners, dtype=jnp.int32)[:, None], 0), axis=0)

    def split_heads(array):
        return array.reshape(1, tok_rows, groups, heads_here, HEAD_DIM)

    query_part = lax.all_to_all(
        split_heads(queries), "seq", split_axis=2, concat_axis=1, tiled=True
    )
    keys_part = lax.all_to_all(
        split_heads(hit_keys), "seq", split_axis=2, concat_axis=1, tiled=True
    )
    values_part = lax.all_to_all(
        split_heads(hit_values), "seq", split_axis=2, concat_axis=1, tiled=True
    )
    n_heads = query_part.shape[3]

    def one_head(index):
        head_query = lax.dynamic_index_in_dim(query_part, index, 3, keepdims=False)[0, :, 0, :]
        head_keys = lax.dynamic_index_in_dim(keys_part, index, 3, keepdims=False)[0, :, 0, :]
        head_values = lax.dynamic_index_in_dim(values_part, index, 3, keepdims=False)[0, :, 0, :]
        return attend_head(head_query, head_keys, head_values, count)

    outputs = lax.map(one_head, jnp.arange(n_heads, dtype=jnp.int32))
    attended = jnp.moveaxis(outputs, 0, 1)[None, :, None, :, :]
    returned = lax.all_to_all(attended, "seq", split_axis=1, concat_axis=2, tiled=True)
    rows_in = returned.reshape(tok_rows, width)
    owned = lax.all_gather(weight_half, "dp", axis=0, tiled=True)
    full = lax.all_gather(owned, "seq", axis=2, tiled=True)
    projection = jnp.take(full, inverse, axis=0).reshape(width, width)
    total = jnp.dot(rows_in, projection, preferred_element_type=jnp.float32)
    projected = total.astype(jnp.bfloat16)[None]
    return (projected, new_master, new_first, new_second)


def solution(mesh):
    return jax.shard_map(
        body,
        mesh=mesh,
        in_specs=(
            P("dp", "seq", None),
            P("dp", "seq", None),
            P("dp", "seq", None),
            P("dp"),
            P("dp", None, "seq"),
            P("dp", None, "seq"),
            P("dp", None, "seq"),
            P("dp", None, "seq"),
            P(),
        ),
        out_specs=(
            P("dp", "seq", None),
            P("dp", None, "seq"),
            P("dp", None, "seq"),
            P("dp", None, "seq"),
        ),
        check_vma=False,
    )
```

profile of v0, /device:TPU:0, one launch (start us, length us, event | category | flops | bytes accessed | tf_op | source)
XLA Modules:
  0.0 175.6 jit_solution(9775890406966182870)
XLA Ops:
  7.2 3.1 %fusion.15 = (bf16[1,256,512]{2,1,0:T(8,128)(2,1)}, f32[1,256,512]{2,1,0:T(8,128)}, f32[1,256,512]{2,1,0:T(8,128)}, f32[1,256,512]{2,1,0:T(8,128)}) fusion(f32[1,256,512]{2,1,0:T(8,128)} %param.15, f32[1,256,512]{2,1,0:T(8,128)} %param.18, f32[1,256,512]{2,1,0:T(8,128)} %param.16, f32[1,256,512]{2,1,0:T(8,128)} %param.17), kind=kLoop, calls=%fused_computation.33 | loop fusion | flops 2097152 | bytes 3932160 | tf_op jit(solution)/shard_map/convert_element_type | solution.py:66
  10.4 52.3 %all-gather.3.cloned.1.call-done = bf16[8,256,512]{2,1,0:T(8,128)(2,1)} async-done(((bf16[1,256,512]{2,1,0:T(8,128)(2,1)}), bf16[8,256,512]{2,1,0:T(8,128)(2,1)}) %all-gather.3.cloned.1.call-update) | async-done | bytes 2097168 | tf_op jit(solution)/shard_map/all_gather | solution.py:101
  62.8 1.3 copy.41
  64.1 1.0 copy.42
  65.1 3.5 %all-to-all-start.1 = ((bf16[1,128,4,4,128]{4,1,3,0,2:T(8,128)(2,1)}), bf16[1,128,4,4,128]{4,1,3,0,2:T(8,128)(2,1)S(1)}, u32[]{:S(2)}, u32[]{:S(2)}) async-start(bf16[1,128,4,4,128]{4,1,3,0,2:T(8,128)(2,1)} %copy.42), calls=%async_computation.1 | async-start | bytes 1048576 | tf_op jit(solution)/shard_map/all_to_all | solution.py:83
  68.9 1.0 copy.45
  69.9 10.8 %all-to-all-done.1 = bf16[1,128,4,4,128]{4,1,3,0,2:T(8,128)(2,1)S(1)} async-done(((bf16[1,128,4,4,128]{4,1,3,0,2:T(8,128)(2,1)}), bf16[1,128,4,4,128]{4,1,3,0,2:T(8,128)(2,1)S(1)}, u32[]{:S(2)}, u32[]{:S(2)}) %all-to-all-start.1) | async-done | bytes 524320 | tf_op jit(solution)/shard_map/all_to_all | solution.py:83
  80.7 3.5 %all-to-all-start.2 = ((bf16[1,128,4,4,128]{4,1,3,0,2:T(8,128)(2,1)}), bf16[1,128,4,4,128]{4,1,3,0,2:T(8,128)(2,1)S(1)}, u32[]{:S(2)}, u32[]{:S(2)}) async-start(bf16[1,128,4,4,128]{4,1,3,0,2:T(8,128)(2,1)} %copy.45), calls=%async_computation.2 | async-start | bytes 1048576 | tf_op jit(solution)/shard_map/all_to_all | solution.py:86
  84.5 1.0 copy.39
  85.5 13.4 %all-to-all-done.2 = bf16[1,128,4,4,128]{4,1,3,0,2:T(8,128)(2,1)S(1)} async-done(((bf16[1,128,4,4,128]{4,1,3,0,2:T(8,128)(2,1)}), bf16[1,128,4,4,128]{4,1,3,0,2:T(8,128)(2,1)S(1)}, u32[]{:S(2)}, u32[]{:S(2)}) %all-to-all-start.2) | async-done | bytes 524320 | tf_op jit(solution)/shard_map/all_to_all | solution.py:86
  99.0 3.5 %all-to-all-start = ((bf16[1,128,4,4,128]{4,1,3,0,2:T(8,128)(2,1)}), bf16[1,128,4,4,128]{4,1,3,0,2:T(8,128)(2,1)S(1)}, u32[]{:S(2)}, u32[]{:S(2)}) async-start(bf16[1,128,4,4,128]{4,1,3,0,2:T(8,128)(2,1)} %copy.39), calls=%async_computation | async-start | bytes 1048576 | tf_op jit(solution)/shard_map/all_to_all | solution.py:80
  102.6 14.5 %all-to-all-done = bf16[1,128,4,4,128]{4,1,3,0,2:T(8,128)(2,1)S(1)} async-done(((bf16[1,128,4,4,128]{4,1,3,0,2:T(8,128)(2,1)}), bf16[1,128,4,4,128]{4,1,3,0,2:T(8,128)(2,1)S(1)}, u32[]{:S(2)}, u32[]{:S(2)}) %all-to-all-start) | async-done | bytes 524320 | tf_op jit(solution)/shard_map/all_to_all | solution.py:80
  117.2 16.6 %while.10 = (s32[]{:T(128)}, bf16[4,512,128]{2,1,0:T(8,128)(2,1)S(1)}, s32[]{:T(128)}, s32[4]{0:T(128)S(1)}, bf16[1,512,1,4,128]{4,1,3,2,0:T(8,128)(2,1)S(1)}, /...) while((s32[]{:T(128)}, ...), condition=%wide.region_3.4_spmd, body=%wide.region_0.3_spmd.sunk | while | flops 136379904 | bytes 3682463 | solution.py:97
  117.3 0.6 dynamic_slice.40
  119.8 0.7 iota_compare_fusion.3
  123.9 0.7 iota_compare_fusion.3
  128.1 0.7 iota_compare_fusion.3
  132.3 0.7 iota_compare_fusion.3
  133.9 1.2 copy.51
  135.1 3.5 %all-to-all-start.3 = ((bf16[1,512,1,4,128]{4,3,2,0,1:T(4,128)(2,1)}), bf16[1,512,1,4,128]{4,3,2,0,1:T(4,128)(2,1)S(1)}, u32[]{:S(2)}, u32[]{:S(2)}) async-start(bf16[1,512,1,4,128]{4,3,2,0,1:T(4,128)(2,1)} %bitcast.54), calls=%async_computation.3 | async-start | bytes 1048576 | tf_op jit(solution)/shard_map/all_to_all | solution.py:99
  138.6 8.8 %all-to-all-done.3 = bf16[1,512,1,4,128]{4,3,2,0,1:T(4,128)(2,1)S(1)} async-done(((bf16[1,512,1,4,128]{4,3,2,0,1:T(4,128)(2,1)}), bf16[1,512,1,4,128]{4,3,2,0,1:T(4,128)(2,1)S(1)}, u32[]{:S(2)}, u32[]{:S(2)}) %all-to-all-start.3) | async-done | bytes 524320 | tf_op jit(solution)/shard_map/all_to_all | solution.py:99
  147.8 8.1 %gather_fusion = bf16[8,256,2048]{2,1,0:T(8,128)(2,1)} fusion(bf16[8,256,2048]{2,1,0:T(8,128)(2,1)} %all-gather.5.cloned.1.call-done, s32[1024]{0:T(1024)S(1)} %pad_clamp_fusion), kind=kCustom, calls=%fused_computation | custom fusion | bytes 16777248 | tf_op jit(solution)/shard_map/jit(_take)/gather | solution.py:103
  155.8 7.5 %broadcast_select_fusion = bf16[8,256,2048]{2,1,0:T(8,128)(2,1)} fusion(bf16[8,256,2048]{2,1,0:T(8,128)(2,1)} %gather_fusion, pred[8]{0:T(512)(128)(4,1)S(1)} %compare_and_fusion), kind=kLoop, calls=%fused_computation.18 | loop fusion | flops 4194304 | bytes 16777224 | tf_op jit(solution)/shard_map/jit(_take)/select_n | solution.py:103
  163.3 5.5 %fusion.12 = bf16[1,128,2048]{2,1,0:T(8,128)(2,1)} fusion(bf16[128,2048]{0,1:T(8,128)(2,1)S(1)} %bitcast.66, bf16[2048,2048]{1,0:T(8,128)(2,1)} %bitcast.65), kind=kOutput, calls=%fused_computation.20 | convolution fusion | flops 1074003968 | bytes 9437184 | tf_op jit(solution)/shard_map/dot_general | solution.py:104
  (39 shorter events, 6.8 us)
Async XLA Ops:
  7.2 61.4 %copy-start = (bf16[1,128,2048]{2,1,0:T(8,128)(2,1)S(1)}, bf16[1,128,2048]{2,1,0:T(8,128)(2,1)}, u32[]{:S(2)}) copy-start(bf16[1,128,2048]{2,1,0:T(8,128)(2,1)} %param.13) | copy-start | bytes 1572868
  7.2 77.0 %copy-start.1 = (bf16[1,128,2048]{2,1,0:T(8,128)(2,1)S(1)}, bf16[1,128,2048]{2,1,0:T(8,128)(2,1)}, u32[]{:S(2)}) copy-start(bf16[1,128,2048]{2,1,0:T(8,128)(2,1)} %param.11) | copy-start | bytes 1572868
  7.2 95.3 %copy-start.2 = (s32[8]{0:T(128)S(1)}, s32[8]{0:T(128)}, u32[]{:S(2)}) copy-start(s32[8]{0:T(128)} %param.19) | copy-start | bytes 100
  7.2 55.6 %all-gather.3.cloned.1.call-start = ((), (), s32[]{:S(2)}) async-start(), calls=%async_computation.4 | async-start | bytes 2359296 | tf_op jit(solution)/shard_map/all_gather | solution.py:101
  10.4 137.4 %all-gather.5.cloned.1.call-start = ((), (), s32[]{:S(2)}) async-start(), calls=%async_computation.5 | async-start | bytes 10485760 | tf_op jit(solution)/shard_map/all_gather | solution.py:102
  65.1 15.6 %all-to-all-start.1 = ((bf16[1,128,4,4,128]{4,1,3,0,2:T(8,128)(2,1)}), bf16[1,128,4,4,128]{4,1,3,0,2:T(8,128)(2,1)S(1)}, u32[]{:S(2)}, u32[]{:S(2)}) async-start(bf16[1,128,4,4,128]{4,1,3,0,2:T(8,128)(2,1)} %copy.42), calls=%async_computation.1 | async-start | bytes 1048576 | tf_op jit(solution)/shard_map/all_to_all | solution.py:83
  80.7 18.2 %all-to-all-start.2 = ((bf16[1,128,4,4,128]{4,1,3,0,2:T(8,128)(2,1)}), bf16[1,128,4,4,128]{4,1,3,0,2:T(8,128)(2,1)S(1)}, u32[]{:S(2)}, u32[]{:S(2)}) async-start(bf16[1,128,4,4,128]{4,1,3,0,2:T(8,128)(2,1)} %copy.45), calls=%async_computation.2 | async-start | bytes 1048576 | tf_op jit(solution)/shard_map/all_to_all | solution.py:86
  99.0 18.2 %all-to-all-start = ((bf16[1,128,4,4,128]{4,1,3,0,2:T(8,128)(2,1)}), bf16[1,128,4,4,128]{4,1,3,0,2:T(8,128)(2,1)S(1)}, u32[]{:S(2)}, u32[]{:S(2)}) async-start(bf16[1,128,4,4,128]{4,1,3,0,2:T(8,128)(2,1)} %copy.39), calls=%async_computation | async-start | bytes 1048576 | tf_op jit(solution)/shard_map/all_to_all | solution.py:80
  135.1 12.3 %all-to-all-start.3 = ((bf16[1,512,1,4,128]{4,3,2,0,1:T(4,128)(2,1)}), bf16[1,512,1,4,128]{4,3,2,0,1:T(4,128)(2,1)S(1)}, u32[]{:S(2)}, u32[]{:S(2)}) async-start(bf16[1,512,1,4,128]{4,3,2,0,1:T(4,128)(2,1)} %bitcast.54), calls=%async_computation.3 | async-start | bytes 1048576 | tf_op jit(solution)/shard_map/all_to_all | solution.py:99
Sparse Core Ops, SparseCore 0:
  10.7 51.9 all-gather.2
  64.3 71.0 all-gather.4
where the time goes:
time: 176 us
  waiting for transfers between devices  100 us (57%)
  local copies, waits for them, and re-layouts  17 us (10%)
  between operations  14.2 us (8%)
  other arithmetic  14.1 us (8%)
  starting transfers between devices  14 us (8%)
  matrix products  8.47 us (5%)
  loops' own time  7.88 us (4%)
    all_gather x1, waiting for transfers between devices, body(): owned = lax.all_gather(weight_half, 'dp', axis=0, tiled=True)  52.3 us
    all_to_all x1, waiting for transfers between devices, body(): lax.all_to_all(split_heads(queries), 'seq', split_axis=2, concat_axis=1,...  14.5 us
    all_to_all x1, waiting for transfers between devices, body(): lax.all_to_all(split_heads(hit_values), 'seq', split_axis=2, concat_axis=...  13.4 us
    all_to_all x1, waiting for transfers between devices, body(): lax.all_to_all(split_heads(hit_keys), 'seq', split_axis=2, concat_axis=1,...  10.8 us
    all_to_all x1, waiting for transfers between devices, body(): lax.all_to_all(attended, 'seq', split_axis=1, concat_axis=2, tiled=True)  8.77 us
    gather x1, local copies, waits for them, and re-layouts, body(): projection = jnp.take(full, inverse, axis=0).reshape(width, width)  8.08 us
    another operation x1, loops' own time, body(): outputs = lax.map(one_head, jnp.arange(n_heads, dtype=jnp.int32))  7.88 us
    select_n x2, other arithmetic, body(): projection = jnp.take(full, inverse, axis=0).reshape(width, width)  7.49 us
  transfers between devices with their start and end apart: 6, of which 5 were waited for; matrix products, arithmetic and copies ran while one was open for 9% of the time, Pallas kernels for 0%

commit v1 on v0

--- a/solution.py
+++ b/solution.py
@@ -96,7 +96,10 @@
 
     outputs = lax.map(one_head, jnp.arange(n_heads, dtype=jnp.int32))
     attended = jnp.moveaxis(outputs, 0, 1)[None, :, None, :, :]
-    returned = lax.all_to_all(attended, "seq", split_axis=1, concat_axis=2, tiled=True)
+    size = lax.axis_size("seq")
+    pieces = jnp.stack(jnp.split(attended, size, axis=1), axis=0)
+    pieces = lax.all_to_all(pieces, "seq", split_axis=0, concat_axis=0)
+    returned = jnp.concatenate(pieces, axis=2)
     rows_in = returned.reshape(tok_rows, width)
     owned = lax.all_gather(weight_half, "dp", axis=0, tiled=True)
     full = lax.all_gather(owned, "seq", axis=2, tiled=True)

time: 176 us -> 167 us (0.949)
  waiting for transfers between devices: 100 us -> 91.2 us
    all_to_all x1, waiting for transfers between devices: 8.77 us -> 0.01 us  [body(): pieces = lax.all_to_all(pieces, 'seq', split_axis=0, concat_axis=0)]
    all_to_all x1, waiting for transfers between devices: 14.5 us -> 10.8 us  [body(): lax.all_to_all(split_heads(queries), 'seq', split_axis=2, concat_axis=1,...]
    all_to_all x1, waiting for transfers between devices: 10.8 us -> 13.4 us  [body(): lax.all_to_all(split_heads(hit_keys), 'seq', split_axis=2, concat_axis=1,...]
  transfers between devices with their start and end apart: 6 -> 6, of which waited for: 5 -> 4; matrix products, arithmetic and copies ran while one was open for 9% -> 18% of each run, Pallas kernels for 0% -> 0%
where the time goes in v1:
time: 167 us
  waiting for transfers between devices  91.2 us (55%)
  local copies, waits for them, and re-layouts  16.1 us (10%)
  other arithmetic  14.9 us (9%)
  between operations  14.2 us (9%)
  starting transfers between devices  14 us (8%)
  matrix products  8.24 us (5%)
  loops' own time  7.97 us (5%)
    all_gather x1, waiting for transfers between devices, body(): owned = lax.all_gather(weight_half, 'dp', axis=0, tiled=True)  52.3 us
    all_to_all x1, waiting for transfers between devices, body(): lax.all_to_all(split_heads(hit_values), 'seq', split_axis=2, concat_axis=...  14.6 us
    all_to_all x1, waiting for transfers between devices, body(): lax.all_to_all(split_heads(hit_keys), 'seq', split_axis=2, concat_axis=1,...  13.4 us
    all_to_all x1, waiting for transfers between devices, body(): lax.all_to_all(split_heads(queries), 'seq', split_axis=2, concat_axis=1,...  10.8 us
    gather x1, local copies, waits for them, and re-layouts, body(): projection = jnp.take(full, inverse, axis=0).reshape(width, width)  8.07 us
    another operation x1, loops' own time, body(): outputs = lax.map(one_head, jnp.arange(n_heads, dtype=jnp.int32))  7.97 us
    select_n x2, other arithmetic, body(): projection = jnp.take(full, inverse, axis=0).reshape(width, width)  7.48 us
    dot_general x1, matrix products, body(): total = jnp.dot(rows_in, projection, preferred_element_type=jnp.float32)  5.46 us
  transfers between devices with their start and end apart: 6, of which 4 were waited for; matrix products, arithmetic and copies ran while one was open for 18% of the time, Pallas kernels for 0%

profile of v1, /device:TPU:0, one launch (start us, length us, event | category | flops | bytes accessed | tf_op | source)
XLA Modules:
  0.0 166.6 jit_solution(13997543822994115507)
XLA Ops:
  7.2 3.1 %fusion.14 = (bf16[1,256,512]{2,1,0:T(8,128)(2,1)}, f32[1,256,512]{2,1,0:T(8,128)}, f32[1,256,512]{2,1,0:T(8,128)}, f32[1,256,512]{2,1,0:T(8,128)}) fusion(f32[1,256,512]{2,1,0:T(8,128)} %param.15, f32[1,256,512]{2,1,0:T(8,128)} %param.18, f32[1,256,512]{2,1,0:T(8,128)} %param.16, f32[1,256,512]{2,1,0:T(8,128)} %param.17), kind=kLoop, calls=%fused_computation.37 | loop fusion | flops 2097152 | bytes 3932160 | tf_op jit(solution)/shard_map/convert_element_type | solution.py:66
  10.4 52.3 %all-gather.3.cloned.1.call-done = bf16[8,256,512]{2,1,0:T(8,128)(2,1)} async-done(((bf16[1,256,512]{2,1,0:T(8,128)(2,1)}), bf16[8,256,512]{2,1,0:T(8,128)(2,1)}) %all-gather.3.cloned.1.call-update) | async-done | bytes 2097168 | tf_op jit(solution)/shard_map/all_gather | solution.py:104
  62.8 1.3 copy.36
  64.1 1.0 copy.37
  65.1 3.5 %all-to-all-start = ((bf16[1,128,4,4,128]{4,1,3,0,2:T(8,128)(2,1)}), bf16[1,128,4,4,128]{4,1,3,0,2:T(8,128)(2,1)S(1)}, u32[]{:S(2)}, u32[]{:S(2)}) async-start(bf16[1,128,4,4,128]{4,1,3,0,2:T(8,128)(2,1)} %copy.37), calls=%async_computation | async-start | bytes 1048576 | tf_op jit(solution)/shard_map/all_to_all | solution.py:80
  68.9 1.0 copy.40
  69.9 10.8 %all-to-all-done = bf16[1,128,4,4,128]{4,1,3,0,2:T(8,128)(2,1)S(1)} async-done(((bf16[1,128,4,4,128]{4,1,3,0,2:T(8,128)(2,1)}), bf16[1,128,4,4,128]{4,1,3,0,2:T(8,128)(2,1)S(1)}, u32[]{:S(2)}, u32[]{:S(2)}) %all-to-all-start) | async-done | bytes 524320 | tf_op jit(solution)/shard_map/all_to_all | solution.py:80
  80.7 3.5 %all-to-all-start.1 = ((bf16[1,128,4,4,128]{4,1,3,0,2:T(8,128)(2,1)}), bf16[1,128,4,4,128]{4,1,3,0,2:T(8,128)(2,1)S(1)}, u32[]{:S(2)}, u32[]{:S(2)}) async-start(bf16[1,128,4,4,128]{4,1,3,0,2:T(8,128)(2,1)} %copy.40), calls=%async_computation.1 | async-start | bytes 1048576 | tf_op jit(solution)/shard_map/all_to_all | solution.py:83
  84.5 1.0 copy.43
  85.6 13.4 %all-to-all-done.1 = bf16[1,128,4,4,128]{4,1,3,0,2:T(8,128)(2,1)S(1)} async-done(((bf16[1,128,4,4,128]{4,1,3,0,2:T(8,128)(2,1)}), bf16[1,128,4,4,128]{4,1,3,0,2:T(8,128)(2,1)S(1)}, u32[]{:S(2)}, u32[]{:S(2)}) %all-to-all-start.1) | async-done | bytes 524320 | tf_op jit(solution)/shard_map/all_to_all | solution.py:83
  99.0 3.5 %all-to-all-start.2 = ((bf16[1,128,4,4,128]{4,1,3,0,2:T(8,128)(2,1)}), bf16[1,128,4,4,128]{4,1,3,0,2:T(8,128)(2,1)S(1)}, u32[]{:S(2)}, u32[]{:S(2)}) async-start(bf16[1,128,4,4,128]{4,1,3,0,2:T(8,128)(2,1)} %copy.43), calls=%async_computation.2 | async-start | bytes 1048576 | tf_op jit(solution)/shard_map/all_to_all | solution.py:86
  102.6 14.6 %all-to-all-done.2 = bf16[1,128,4,4,128]{4,1,3,0,2:T(8,128)(2,1)S(1)} async-done(((bf16[1,128,4,4,128]{4,1,3,0,2:T(8,128)(2,1)}), bf16[1,128,4,4,128]{4,1,3,0,2:T(8,128)(2,1)S(1)}, u32[]{:S(2)}, u32[]{:S(2)}) %all-to-all-start.2) | async-done | bytes 524320 | tf_op jit(solution)/shard_map/all_to_all | solution.py:86
  117.2 17.0 %while.10 = (s32[]{:T(128)}, bf16[4,512,128]{1,2,0:T(8,128)(2,1)S(1)}, s32[]{:T(128)}, s32[4]{0:T(128)S(1)}, bf16[1,512,1,4,128]{4,1,3,2,0:T(8,128)(2,1)S(1)}, /...) while((s32[]{:T(128)}, ...), condition=%wide.region_3.4_spmd, body=%wide.region_0.3_spmd.sunk | while | flops 136379904 | bytes 4206759 | solution.py:97
  117.3 0.6 dynamic_slice.40
  119.8 0.7 iota_compare_fusion.3
  121.5 0.6 dynamic_slice.40
  124.0 0.7 iota_compare_fusion.3
  128.3 0.7 iota_compare_fusion.3
  132.5 0.7 iota_compare_fusion.3
  134.4 0.9 pad_maximum_fusion
  135.3 3.5 %all-to-all-start.3 = ((bf16[4,1,128,1,4,128]{2,5,4,3,1,0:T(8,128)(2,1)}), bf16[4,1,128,1,4,128]{2,5,4,3,1,0:T(8,128)(2,1)S(1)}, u32[]{:S(2)}, u32[]{:S(2)}) async-start(bf16[4,1,128,1,4,128]{2,5,4,3,1,0:T(8,128)(2,1)} %pad_maximum_fusion), calls=%async_computation.3 | async-start | bytes 1048576 | tf_op jit(solution)/shard_map/all_to_all | solution.py:101
  138.8 8.1 %gather_fusion = bf16[8,256,2048]{2,1,0:T(8,128)(2,1)} fusion(bf16[8,256,2048]{2,1,0:T(8,128)(2,1)} %all-gather.5.cloned.1.call-done, s32[1024]{0:T(1024)S(1)} %pad_clamp_fusion), kind=kCustom, calls=%fused_computation | custom fusion | bytes 16777248 | tf_op jit(solution)/shard_map/jit(_take)/gather | solution.py:106
  146.8 7.5 %broadcast_select_fusion = bf16[8,256,2048]{2,1,0:T(8,128)(2,1)} fusion(bf16[8,256,2048]{2,1,0:T(8,128)(2,1)} %gather_fusion, pred[8]{0:T(512)(128)(4,1)S(1)} %compare_and_fusion), kind=kLoop, calls=%fused_computation.18 | loop fusion | flops 4194304 | bytes 16777224 | tf_op jit(solution)/shard_map/jit(_take)/select_n | solution.py:106
  154.3 5.5 %fusion.11 = bf16[1,128,2048]{2,1,0:T(8,128)(2,1)} fusion(bf16[128,2048]{0,1:T(8,128)(2,1)S(1)} %bitcast.71, bf16[2048,2048]{1,0:T(8,128)(2,1)} %bitcast.70), kind=kOutput, calls=%fused_computation.20 | convolution fusion | flops 1074003968 | bytes 9437184 | tf_op jit(solution)/shard_map/dot_general | solution.py:107
  (46 shorter events, 6.3 us)
Async XLA Ops:
  7.2 61.4 %copy-start = (bf16[1,128,2048]{2,1,0:T(8,128)(2,1)S(1)}, bf16[1,128,2048]{2,1,0:T(8,128)(2,1)}, u32[]{:S(2)}) copy-start(bf16[1,128,2048]{2,1,0:T(8,128)(2,1)} %param.12) | copy-start | bytes 1572868
  7.2 77.0 %copy-start.1 = (bf16[1,128,2048]{2,1,0:T(8,128)(2,1)S(1)}, bf16[1,128,2048]{2,1,0:T(8,128)(2,1)}, u32[]{:S(2)}) copy-start(bf16[1,128,2048]{2,1,0:T(8,128)(2,1)} %param.13) | copy-start | bytes 1572868
  7.2 78.3 %copy-start.2 = (s32[8]{0:T(128)S(1)}, s32[8]{0:T(128)}, u32[]{:S(2)}) copy-start(s32[8]{0:T(128)} %param.19) | copy-start | bytes 100
  7.2 55.6 %all-gather.3.cloned.1.call-start = ((), (), s32[]{:S(2)}) async-start(), calls=%async_computation.4 | async-start | bytes 2359296 | tf_op jit(solution)/shard_map/all_gather | solution.py:104
  10.4 128.4 %all-gather.5.cloned.1.call-start = ((), (), s32[]{:S(2)}) async-start(), calls=%async_computation.5 | async-start | bytes 10485760 | tf_op jit(solution)/shard_map/all_gather | solution.py:105
  65.1 15.6 %all-to-all-start = ((bf16[1,128,4,4,128]{4,1,3,0,2:T(8,128)(2,1)}), bf16[1,128,4,4,128]{4,1,3,0,2:T(8,128)(2,1)S(1)}, u32[]{:S(2)}, u32[]{:S(2)}) async-start(bf16[1,128,4,4,128]{4,1,3,0,2:T(8,128)(2,1)} %copy.37), calls=%async_computation | async-start | bytes 1048576 | tf_op jit(solution)/shard_map/all_to_all | solution.py:80
  80.7 18.2 %all-to-all-start.1 = ((bf16[1,128,4,4,128]{4,1,3,0,2:T(8,128)(2,1)}), bf16[1,128,4,4,128]{4,1,3,0,2:T(8,128)(2,1)S(1)}, u32[]{:S(2)}, u32[]{:S(2)}) async-start(bf16[1,128,4,4,128]{4,1,3,0,2:T(8,128)(2,1)} %copy.40), calls=%async_computation.1 | async-start | bytes 1048576 | tf_op jit(solution)/shard_map/all_to_all | solution.py:83
  99.0 18.2 %all-to-all-start.2 = ((bf16[1,128,4,4,128]{4,1,3,0,2:T(8,128)(2,1)}), bf16[1,128,4,4,128]{4,1,3,0,2:T(8,128)(2,1)S(1)}, u32[]{:S(2)}, u32[]{:S(2)}) async-start(bf16[1,128,4,4,128]{4,1,3,0,2:T(8,128)(2,1)} %copy.43), calls=%async_computation.2 | async-start | bytes 1048576 | tf_op jit(solution)/shard_map/all_to_all | solution.py:86
  135.3 19.1 %all-to-all-start.3 = ((bf16[4,1,128,1,4,128]{2,5,4,3,1,0:T(8,128)(2,1)}), bf16[4,1,128,1,4,128]{2,5,4,3,1,0:T(8,128)(2,1)S(1)}, u32[]{:S(2)}, u32[]{:S(2)}) async-start(bf16[4,1,128,1,4,128]{2,5,4,3,1,0:T(8,128)(2,1)} %pad_maximum_fusion), calls=%async_computation.3 | async-start | bytes 1048576 | tf_op jit(solution)/shard_map/all_to_all | solution.py:101
Sparse Core Ops, SparseCore 0:
  10.7 51.9 all-gather.2
  64.3 71.0 all-gather.4
